TPU v7x, 256 devices: a whole 4x4x8 slice. The times are simulated.
256 devices in a mesh: node: 64 (over z, y, core), state: 4 (over x).
Axes of the slice: x: 4, y: 4, z: 8, core: 2. Of those that a mesh axis runs over, the one named last changes fastest.
Arguments:
- block: bfloat16 [64, 2097152], P('state', 'node'), may hold values from -6 to 6
- connectivity: int32 [125, 32768], P(None, 'node'), may hold values from 0 to 49151, as said below
- potential: float32 [125, 32768], P(None, 'node'), may hold values from 0.1 to 3
- cell_matrix: bfloat16 [125, 125], replicated, as said below
Outputs:
- orthonormal: bfloat16 [64, 2097152], P('state', 'node')
- factor: float32 [64, 64], replicated
Inputs may be any that keep to these rules, and one draw needn't show every extreme that they name: `connectivity`: in each slab, numbers below 8192 are the previous slab's last 8192 nodes and numbers from 40960 on are the next slab's first nodes. The numbers of the slab's k-th cell (k from 0) lie in k * 96 to k * 96 + 2 * 96 - 1, those of its last cell in k * 96 to k * 96 + 95; each cell reaches the lower end of its range. `cell_matrix`: Symmetric.
All inputs are finite; a program needn't handle non-finite values.
Results may differ from a plain program's by a relative error of at most 0.015.
Values may be sent and summed in bfloat16 or wider, within the bound.
No kernel may reach another device: no remote copies, remote signals or barrier semaphores. Data moves between devices by JAX's collectives and lax.ppermute only.
A program may use at most 64 MiB of HBM per device.

v0:
```python
import jax
import jax.numpy as jnp
from jax import lax
from jax.sharding import PartitionSpec as P

CENTER = 3.0
HALF_WIDTH = 3.0


def extended(block, sides, width):
    for axis, dim in sides:
        count = lax.axis_size(axis)
        forward = [(i, i + 1) for i in range(count - 1)]
        backward = [(target, source) for source, target in forward]
        low = lax.ppermute(
            lax.slice_in_dim(block, block.shape[dim] - width, None, axis=dim), axis, forward
        )
        high = lax.ppermute(lax.slice_in_dim(block, 0, width, axis=dim), axis, backward)
        block = jnp.concatenate([low, block, high], axis=dim)
    return block


def passed_along(block, axis, distance):
    devices = range(lax.axis_size(axis))
    route = [(i - distance, i) for i in devices if i - distance in devices]
    return lax.ppermute(block, axis, route)


def cell_terms(window, connectivity, potential, cell_matrix):
    states = window.shape[0]
    cells = connectivity.shape[1]
    stride = window.shape[1] // cells
    segments = window.reshape(states, cells, stride)
    following = jnp.concatenate(
        [segments[:, 1:], jnp.zeros((states, 1, stride), segments.dtype)], axis=1
    )
    paired = jnp.concatenate([segments, following], axis=2)
    offsets = jnp.arange(cells, dtype=jnp.int32) * stride
    local_links = connectivity - offsets[None, :]
    columns = jnp.arange(2 * stride, dtype=jnp.int32)
    group = min(cells, 128)
    pieces = []
    for first_cell in range(0, cells, group):
        links = local_links[:, first_cell : first_cell + group]
        picker = links[:, :, None] == columns[None, None, :]
        picker_half = picker.astype(jnp.bfloat16)
        part_pair = paired[:, first_cell : first_cell + group]
        values = jnp.einsum(
            "skn,jkn->sjk", part_pair, picker_half, preferred_element_type=jnp.float32
        )
        mixed = jnp.einsum(
            "ij,sjk->sik",
            cell_matrix,
            values.astype(jnp.bfloat16),
            preferred_element_type=jnp.float32,
        )
        mixed = mixed + potential[None, :, first_cell : first_cell + group] * values
        spread = jnp.einsum(
            "sjk,jkn->skn", mixed, picker.astype(jnp.float32), precision=lax.Precision.HIGHEST
        )
        pieces.append(spread)
    spread = jnp.concatenate(pieces, axis=1)
    lower = spread[:, :, :stride]
    upper = spread[:, :, stride:]
    shifted = jnp.concatenate([jnp.zeros((states, 1, stride), jnp.float32), upper[:, :-1]], axis=1)
    return (lower + shifted).reshape(states, cells * stride)


def operate(field, connectivity, potential, cell_matrix):
    owned = field.shape[1]
    margin = owned // 4
    window = extended(field, (("node", 1),), margin)
    summed = cell_terms(window, connectivity, potential, cell_matrix)
    result = summed[:, margin : margin + owned]
    from_above = passed_along(summed[:, :margin].astype(jnp.bfloat16), "node", -1).astype(
        jnp.float32
    )
    from_below = passed_along(summed[:, margin + owned :].astype(jnp.bfloat16), "node", 1).astype(
        jnp.float32
    )
    result = result.at[:, owned - margin :].add(from_above)
    result = result.at[:, :margin].add(from_below)
    return result


def factorize(intersection):
    factor = jnp.linalg.cholesky(intersection)
    identity = jnp.eye(intersection.shape[0], dtype=factor.dtype)
    inverse = lax.linalg.triangular_solve(factor, identity, left_side=True, lower=True).astype(
        jnp.bfloat16
    )
    return (factor, inverse)


def per_device(block, connectivity, potential, cell_matrix):
    start = block.astype(jnp.float32)
    image = operate(block, connectivity, potential, cell_matrix)
    first = ((image - CENTER * start) / HALF_WIDTH).astype(jnp.bfloat16)
    image = operate(first, connectivity, potential, cell_matrix)
    second = (2.0 * (image - CENTER * first.astype(jnp.float32)) / HALF_WIDTH - start).astype(
        jnp.bfloat16
    )
    total_nodes = block.shape[1] * lax.axis_size("node")
    panel = lax.all_gather(second, "state", axis=0, tiled=True)
    partial_intersection = jnp.einsum("an,bn->ab", panel, panel, preferred_element_type=jnp.float32)
    intersection = lax.psum(partial_intersection, "node") / total_nodes
    factor, inverse = factorize(intersection)
    rows = second.shape[0]
    mine = lax.dynamic_slice_in_dim(inverse, lax.axis_index("state") * rows, rows, 0)
    orthonormal = jnp.dot(mine, panel, preferred_element_type=jnp.float32).astype(jnp.bfloat16)
    return (orthonormal, factor)


def solution(mesh):
    return jax.shard_map(
        per_device,
        mesh=mesh,
        in_specs=(P("state", "node"), P(None, "node"), P(None, "node"), P()),
        out_specs=(P("state", "node"), P()),
        check_vma=False,
    )
```

profile of v0, /device:TPU:2, one launch (start us, length us, event | category | flops | bytes accessed | tf_op | source)
XLA Modules:
  0.0 566.9 jit_solution(16091128970053678684)
XLA Ops:
  16.8 3.2 reshape.132
  24.5 3.0 fusion.123
  28.4 4.3 fusion.122
  33.6 4.3 fusion.121
  39.8 4.2 fusion.120
  45.8 11.6 %fusion.42 = f32[16,128,192]{2,0,1:T(8,128)S(1)} fusion(s32[125,128]{0,1:T(8,128)S(1)} %copy.16, f32[16,128,125]{2,0,1:T(8,128)S(1)} %copy.33, f32[16,125,128]{1,0,2:T(8,128)} %get-tuple-element.75, f32[125,128]{0,1:T(8,128)} %copy.19), kind=kOutput, calls=%fused_computation.59 | convolution fusion | flops 593408000 | bytes 3748864 | tf_op jit(solution)/shard_map/sjk,jkn->skn/dot_general | solution.py:58
  57.4 9.9 %fusion.44 = f32[16,128,192]{2,0,1:T(8,128)S(1)} fusion(s32[125,128]{0,1:T(8,128)S(1)} %copy-done.11, f32[16,128,125]{2,0,1:T(8,128)S(1)} %copy.35, f32[16,125,128]{1,0,2:T(8,128)S(1)} %copy-done.19, f32[125,128]{0,1:T(8,128)S(1)} %copy-done.14), kind=kOutput, calls=%fused_computation.61 | convolution fusion | flops 593408000 | bytes 3748864 | tf_op jit(solution)/shard_map/sjk,jkn->skn/dot_general | solution.py:58
  67.3 10.0 %fusion.46 = f32[16,128,192]{2,0,1:T(8,128)S(1)} fusion(s32[125,128]{0,1:T(8,128)S(1)} %copy.22, f32[16,128,125]{2,0,1:T(8,128)S(1)} %copy-done.7, f32[16,125,128]{1,0,2:T(8,128)S(1)} %copy-done.20, f32[125,128]{0,1:T(8,128)S(1)} %copy.23), kind=kOutput, calls=%fused_computation.63 | convolution fusion | flops 593408000 | bytes 3748864 | tf_op jit(solution)/shard_map/sjk,jkn->skn/dot_general | solution.py:58
  77.3 9.8 %fusion.48 = f32[16,128,192]{2,0,1:T(8,128)S(1)} fusion(s32[125,128]{0,1:T(8,128)S(1)} %copy.24, f32[16,128,125]{2,0,1:T(8,128)S(1)} %copy-done.9, f32[16,125,128]{1,0,2:T(8,128)S(1)} %copy-done.21, f32[125,128]{0,1:T(8,128)S(1)} %copy.25), kind=kOutput, calls=%fused_computation.65 | convolution fusion | flops 593408000 | bytes 3748864 | tf_op jit(solution)/shard_map/sjk,jkn->skn/dot_general | solution.py:58
  90.5 3.2 copy.26
  93.8 4.0 reshape.133
  100.0 6.8 %collective-permute-start.3 = (bf16[16,8192]{1,0:T(8,128)(2,1)S(1)}, bf16[16,8192]{1,0:T(8,128)(2,1)S(1)}, u32[]{:S(2)}, u32[]{:S(2)}) collective-permute-start(bf16[16,8192]{1,0:T(8,128)(2,1)S(1)} %get-tuple-element.54), channel_id=1, source_target_pairs={{0,4},{4,8},{8,12},{12,16},{16,20},{20,24},{24,28},{28,32},{32,36}... | collective-permute-start | bytes 786440 | tf_op jit(solution)/shard_map/ppermute | solution.py:26
  109.2 5.8 %collective-permute-start.4 = (bf16[16,8192]{1,0:T(8,128)(2,1)S(1)}, bf16[16,8192]{1,0:T(8,128)(2,1)S(1)}, u32[]{:S(2)}, u32[]{:S(2)}) collective-permute-start(bf16[16,8192]{1,0:T(8,128)(2,1)S(1)} %get-tuple-element.56), channel_id=1, source_target_pairs={{0,4},{4,8},{8,12},{12,16},{16,20},{20,24},{24,28},{28,32},{32,36}... | collective-permute-start | bytes 786440 | tf_op jit(solution)/shard_map/ppermute | solution.py:15
  116.3 4.1 collective-permute-done.5
  121.7 3.2 reshape.134
  129.6 3.0 fusion.127
  132.7 3.0 fusion.126
  135.7 3.0 fusion.125
  138.7 3.0 fusion.124
  147.0 11.7 %fusion.43 = f32[16,128,192]{2,0,1:T(8,128)S(1)} fusion(s32[125,128]{0,1:T(8,128)S(1)} %copy.16, f32[16,128,125]{2,0,1:T(8,128)} %copy.41, f32[16,125,128]{1,0,2:T(8,128)} %get-tuple-element.83, f32[125,128]{0,1:T(8,128)} %copy.19), kind=kOutput, calls=%fused_computation.60 | convolution fusion | flops 593408000 | bytes 3748864 | tf_op jit(solution)/shard_map/sjk,jkn->skn/dot_general | solution.py:58
  158.8 9.9 %fusion.45 = f32[16,128,192]{2,0,1:T(8,128)S(1)} fusion(s32[125,128]{0,1:T(8,128)S(1)} %copy-done.13, f32[16,128,125]{2,0,1:T(8,128)S(1)} %copy-done.8, f32[16,125,128]{1,0,2:T(8,128)S(1)} %copy-done.18, f32[125,128]{0,1:T(8,128)S(1)} %copy-done.15), kind=kOutput, calls=%fused_computation.62 | convolution fusion | flops 593408000 | bytes 3748864 | tf_op jit(solution)/shard_map/sjk,jkn->skn/dot_general | solution.py:58
  168.7 10.0 %fusion.47 = f32[16,128,192]{2,0,1:T(8,128)S(1)} fusion(s32[125,128]{0,1:T(8,128)S(1)} %copy.22, f32[16,128,125]{2,0,1:T(8,128)S(1)} %copy.45, f32[16,125,128]{1,0,2:T(8,128)S(1)} %copy-done.17, f32[125,128]{0,1:T(8,128)S(1)} %copy.23), kind=kOutput, calls=%fused_computation.64 | convolution fusion | flops 593408000 | bytes 3748864 | tf_op jit(solution)/shard_map/sjk,jkn->skn/dot_general | solution.py:58
  178.7 9.8 %fusion.49 = f32[16,128,192]{2,0,1:T(8,128)S(1)} fusion(s32[125,128]{0,1:T(8,128)S(1)} %copy.24, f32[16,128,125]{2,0,1:T(8,128)S(1)} %copy.47, f32[16,125,128]{1,0,2:T(8,128)S(1)} %copy-done.16, f32[125,128]{0,1:T(8,128)S(1)} %copy.25), kind=kOutput, calls=%fused_computation.66 | convolution fusion | flops 593408000 | bytes 3748864 | tf_op jit(solution)/shard_map/sjk,jkn->skn/dot_general | solution.py:58
  192.0 3.2 copy.29
  195.2 4.0 reshape.135
  201.0 7.3 %collective-permute-start.7 = (bf16[16,8192]{1,0:T(8,128)(2,1)S(1)}, bf16[16,8192]{1,0:T(8,128)(2,1)S(1)}, u32[]{:S(2)}, u32[]{:S(2)}) collective-permute-start(bf16[16,8192]{1,0:T(8,128)(2,1)S(1)} %get-tuple-element.52), channel_id=1, source_target_pairs={{0,4},{4,8},{8,12},{12,16},{16,20},{20,24},{24,28},{28,32},{32,36}... | collective-permute-start | bytes 786440 | tf_op jit(solution)/shard_map/ppermute | solution.py:26
  211.7 75.3 %all-gather.2.cloned.1.call-done = bf16[64,32768]{1,0:T(8,128)(2,1)} async-done(((bf16[16,32768]{1,0:T(8,128)(2,1)}), bf16[64,32768]{1,0:T(8,128)(2,1)}) %all-gather.2.cloned.1.call-update) | async-done | bytes 4194320 | tf_op jit(solution)/shard_map/all_gather | solution.py:104
  287.0 4.7 fusion.128
  291.7 251.0 %psum.7 = f32[64,64]{0,1:T(8,128)S(1)} all-reduce(f32[64,64]{0,1:T(8,128)S(1)} %fusion.128), channel_id=1, replica_groups=mesh['node'=64,'state'=4] {'node'}, use_global_device_ids=true, to_apply=%region_1.0 | all-reduce | flops 4096 | bytes 32768 | tf_op jit(solution)/shard_map/psum | solution.py:106
  542.8 5.8 %cholesky.17 = f32[64,64]{1,0:T(8,128)S(1)} custom-call(f32[64,64]{1,0:T(8,128)S(1)} %fusion.104), custom_call_target="Cholesky" | custom-call | tf_op jit(solution)/shard_map/jit(cholesky)/cholesky | solution.py:87
  550.6 4.9 custom-call.6
  555.8 3.8 convolution_convert_fusion
  (120 shorter events, 50.7 us)
Async XLA Ops:
  7.2 20.4 %copy-start = (bf16[125,125]{1,0:T(8,128)(2,1)S(1)}, bf16[125,125]{1,0:T(8,128)(2,1)}, u32[]{:S(2)}) copy-start(bf16[125,125]{1,0:T(8,128)(2,1)} %param.15) | copy-start | bytes 93754
  7.2 8.4 %copy-start.1 = (bf16[16,32768]{1,0:T(8,128)(2,1)S(1)}, bf16[16,32768]{1,0:T(8,128)(2,1)}, u32[]{:S(2)}) copy-start(bf16[16,32768]{1,0:T(8,128)(2,1)} %param.12) | copy-start | bytes 3145732
  7.2 279.8 %all-gather.2.cloned.1.call-start = ((), (), s32[]{:S(2)}) async-start(), calls=%async_computation | async-start | bytes 5242880 | tf_op jit(solution)/shard_map/all_gather | solution.py:104
  8.4 7.1 %collective-permute-start = (bf16[16,8192]{1,0:T(8,128)(2,1)S(1)}, bf16[16,8192]{1,0:T(8,128)(2,1)S(1)}, u32[]{:S(2)}, u32[]{:S(2)}) collective-permute-start(bf16[16,8192]{1,0:T(8,128)(2,1)S(1)} %get-tuple-element.58), channel_id=1, source_target_pairs={{0,4},{4,8},{8,12},{12,16},{16,20},{20,24},{24,28},{28,32},{32,36}... | collective-permute-start | bytes 786440 | tf_op jit(solution)/shard_map/ppermute | solution.py:15
  10.1 5.4 collective-permute-start.1
  14.4 14.1 %copy-start.10 = (s32[125,128]{0,1:T(8,128)}, s32[125,128]{0,1:T(8,128)S(1)}, u32[]{:S(2)}) copy-start(s32[125,128]{0,1:T(8,128)S(1)} %copy.20) | copy-start | bytes 192004
  24.5 3.0 copy-start.6
  45.8 11.6 %copy-start.11 = (s32[125,128]{0,1:T(8,128)S(1)}, s32[125,128]{0,1:T(8,128)}, u32[]{:S(2)}) copy-start(s32[125,128]{0,1:T(8,128)} %copy-done.10) | copy-start | bytes 192004
  45.8 11.6 %copy-start.14 = (f32[125,128]{0,1:T(8,128)S(1)}, f32[125,128]{0,1:T(8,128)}, u32[]{:S(2)}) copy-start(f32[125,128]{0,1:T(8,128)} %copy.21) | copy-start | bytes 192004
  45.8 11.6 %copy-start.19 = (f32[16,125,128]{1,0,2:T(8,128)S(1)}, f32[16,125,128]{1,0,2:T(8,128)}, u32[]{:S(2)}) copy-start(f32[16,125,128]{1,0,2:T(8,128)} %get-tuple-element.73) | copy-start | bytes 3072004
  57.4 9.9 %copy-start.7 = (f32[16,128,125]{2,0,1:T(8,128)S(1)}, f32[16,128,125]{2,0,1:T(8,128)}, u32[]{:S(2)}) copy-start(f32[16,128,125]{2,0,1:T(8,128)} %copy.37) | copy-start | bytes 3072004
  57.4 9.9 %copy-start.20 = (f32[16,125,128]{1,0,2:T(8,128)S(1)}, f32[16,125,128]{1,0,2:T(8,128)}, u32[]{:S(2)}) copy-start(f32[16,125,128]{1,0,2:T(8,128)} %get-tuple-element.71) | copy-start | bytes 3072004
  67.3 10.0 %copy-start.9 = (f32[16,128,125]{2,0,1:T(8,128)S(1)}, f32[16,128,125]{2,0,1:T(8,128)}, u32[]{:S(2)}) copy-start(f32[16,128,125]{2,0,1:T(8,128)} %copy.39) | copy-start | bytes 3072004
  67.3 10.0 %copy-start.21 = (f32[16,125,128]{1,0,2:T(8,128)S(1)}, f32[16,125,128]{1,0,2:T(8,128)}, u32[]{:S(2)}) copy-start(f32[16,125,128]{1,0,2:T(8,128)} %get-tuple-element.69) | copy-start | bytes 3072004
  98.0 8.9 %collective-permute-start.2 = (bf16[16,8192]{1,0:T(8,128)(2,1)S(1)}, bf16[16,8192]{1,0:T(8,128)(2,1)S(1)}, u32[]{:S(2)}, u32[]{:S(2)}) collective-permute-start(bf16[16,8192]{1,0:T(8,128)(2,1)S(1)} %get-tuple-element.55), channel_id=1, source_target_pairs={{4,0},{8,4},{12,8},{16,12},{20,16},{24,20},{28,24},{32,28},{36,32}... | collective-permute-start | bytes 786440 | tf_op jit(solution)/shard_map/ppermute | solution.py:26
  99.9 8.9 %copy-start.2 = (bf16[16,32768]{1,0:T(8,128)(2,1)S(1)}, bf16[16,32768]{1,0:T(8,128)(2,1)}, u32[]{:S(2)}) copy-start(bf16[16,32768]{1,0:T(8,128)(2,1)} %param.12) | copy-start | bytes 3145732
  100.0 8.0 %collective-permute-start.3 = (bf16[16,8192]{1,0:T(8,128)(2,1)S(1)}, bf16[16,8192]{1,0:T(8,128)(2,1)S(1)}, u32[]{:S(2)}, u32[]{:S(2)}) collective-permute-start(bf16[16,8192]{1,0:T(8,128)(2,1)S(1)} %get-tuple-element.54), channel_id=1, source_target_pairs={{0,4},{4,8},{8,12},{12,16},{16,20},{20,24},{24,28},{28,32},{32,36}... | collective-permute-start | bytes 786440 | tf_op jit(solution)/shard_map/ppermute | solution.py:26
  109.2 11.3 %copy-start.4 = (bf16[16,32768]{1,0:T(8,128)(2,1)}, bf16[16,32768]{1,0:T(8,128)(2,1)S(1)}, u32[]{:S(2)}) copy-start(bf16[16,32768]{1,0:T(8,128)(2,1)S(1)} %fusion.40) | copy-start | bytes 3145732
  109.2 7.1 %collective-permute-start.4 = (bf16[16,8192]{1,0:T(8,128)(2,1)S(1)}, bf16[16,8192]{1,0:T(8,128)(2,1)S(1)}, u32[]{:S(2)}, u32[]{:S(2)}) collective-permute-start(bf16[16,8192]{1,0:T(8,128)(2,1)S(1)} %get-tuple-element.56), channel_id=1, source_target_pairs={{0,4},{4,8},{8,12},{12,16},{16,20},{20,24},{24,28},{28,32},{32,36}... | collective-permute-start | bytes 786440 | tf_op jit(solution)/shard_map/ppermute | solution.py:15
  115.0 5.4 collective-permute-start.5
  129.6 3.0 copy-start.12
  147.0 11.7 %copy-start.8 = (f32[16,128,125]{2,0,1:T(8,128)S(1)}, f32[16,128,125]{2,0,1:T(8,128)}, u32[]{:S(2)}) copy-start(f32[16,128,125]{2,0,1:T(8,128)} %copy.43) | copy-start | bytes 3072004
  147.0 11.7 %copy-start.13 = (s32[125,128]{0,1:T(8,128)S(1)}, s32[125,128]{0,1:T(8,128)}, u32[]{:S(2)}) copy-start(s32[125,128]{0,1:T(8,128)} %copy-done.10) | copy-start | bytes 192004
  147.0 11.7 %copy-start.15 = (f32[125,128]{0,1:T(8,128)S(1)}, f32[125,128]{0,1:T(8,128)}, u32[]{:S(2)}) copy-start(f32[125,128]{0,1:T(8,128)} %copy.21) | copy-start | bytes 192004
  147.0 11.7 %copy-start.18 = (f32[16,125,128]{1,0,2:T(8,128)S(1)}, f32[16,125,128]{1,0,2:T(8,128)}, u32[]{:S(2)}) copy-start(f32[16,125,128]{1,0,2:T(8,128)} %get-tuple-element.81) | copy-start | bytes 3072004
  158.8 9.9 %copy-start.17 = (f32[16,125,128]{1,0,2:T(8,128)S(1)}, f32[16,125,128]{1,0,2:T(8,128)}, u32[]{:S(2)}) copy-start(f32[16,125,128]{1,0,2:T(8,128)} %get-tuple-element.79) | copy-start | bytes 3072004
  168.6 10.1 %copy-start.16 = (f32[16,125,128]{1,0,2:T(8,128)S(1)}, f32[16,125,128]{1,0,2:T(8,128)}, u32[]{:S(2)}) copy-start(f32[16,125,128]{1,0,2:T(8,128)} %get-tuple-element.77) | copy-start | bytes 3072004
  199.4 10.9 %copy-start.3 = (bf16[16,32768]{1,0:T(8,128)(2,1)S(1)}, bf16[16,32768]{1,0:T(8,128)(2,1)}, u32[]{:S(2)}) copy-start(bf16[16,32768]{1,0:T(8,128)(2,1)} %param.12) | copy-start | bytes 3145732
  199.4 10.9 %copy-start.5 = (bf16[16,32768]{1,0:T(8,128)(2,1)S(1)}, bf16[16,32768]{1,0:T(8,128)(2,1)}, u32[]{:S(2)}) copy-start(bf16[16,32768]{1,0:T(8,128)(2,1)} %copy-done.4) | copy-start | bytes 3145732
  199.4 8.9 %collective-permute-start.6 = (bf16[16,8192]{1,0:T(8,128)(2,1)S(1)}, bf16[16,8192]{1,0:T(8,128)(2,1)S(1)}, u32[]{:S(2)}, u32[]{:S(2)}) collective-permute-start(bf16[16,8192]{1,0:T(8,128)(2,1)S(1)} %get-tuple-element.53), channel_id=1, source_target_pairs={{4,0},{8,4},{12,8},{16,12},{20,16},{24,20},{28,24},{32,28},{36,32}... | collective-permute-start | bytes 786440 | tf_op jit(solution)/shard_map/ppermute | solution.py:26
  201.0 8.4 %collective-permute-start.7 = (bf16[16,8192]{1,0:T(8,128)(2,1)S(1)}, bf16[16,8192]{1,0:T(8,128)(2,1)S(1)}, u32[]{:S(2)}, u32[]{:S(2)}) collective-permute-start(bf16[16,8192]{1,0:T(8,128)(2,1)S(1)} %get-tuple-element.52), channel_id=1, source_target_pairs={{0,4},{4,8},{8,12},{12,16},{16,20},{20,24},{24,28},{28,32},{32,36}... | collective-permute-start | bytes 786440 | tf_op jit(solution)/shard_map/ppermute | solution.py:26
Sparse Core Ops, SparseCore 0:
  211.9 75.0 all-gather.1
where the time goes:
time: 572 us; the launch traced here: 567 us
  blocking collectives  251 us (44%)
  matrix products  122 us (21%)
  waiting for transfers between devices  81.5 us (14%)
  local copies, waits for them, and re-layouts  37.1 us (6%)
  other arithmetic  33.2 us (6%)
  starting transfers between devices  27 us (5%)
  between operations  15.2 us (3%)
    psum x1, blocking collectives, per_device(): intersection = lax.psum(partial_intersection, 'node') / total_nodes  251 us
    dot_general x8, matrix products, cell_terms(): jnp.einsum('sjk,jkn->skn', mixed, picker.astype(jnp.float32), precision=l...  82.7 us
    all_gather x1, waiting for transfers between devices, per_device(): panel = lax.all_gather(second, 'state', axis=0, tiled=True)  75.3 us
    dot_general x8, matrix products, cell_terms(): jnp.einsum('skn,jkn->sjk', part_pair, picker_half, preferred_element_type...  27.9 us
    ppermute x4, starting transfers between devices, passed_along(): return lax.ppermute(block, axis, route)  16.9 us
  transfers between devices with their start and end apart: 9, of which 4 were waited for; matrix products, arithmetic and copies ran while one was open for 1% of the time, Pallas kernels for 0%

commit v1 on v0

--- a/solution.py
+++ b/solution.py
@@ -101,7 +101,9 @@
         jnp.bfloat16
     )
     total_nodes = block.shape[1] * lax.axis_size("node")
-    panel = lax.all_gather(second, "state", axis=0, tiled=True)
+    panel = jnp.concatenate(
+        lax.all_to_all(jnp.stack([second] * lax.axis_size("state")), "state", 0, 0), axis=0
+    )
     partial_intersection = jnp.einsum("an,bn->ab", panel, panel, preferred_element_type=jnp.float32)
     intersection = lax.psum(partial_intersection, "node") / total_nodes
     factor, inverse = factorize(intersection)

time: 572 us -> 551 us (0.963)
  the two profiles are of different devices: /device:TPU:2 before, /device:TPU:128 now
where the time goes in v1:
time: 551 us; the launch traced here: 546 us
  blocking collectives  247 us (45%)
  matrix products  122 us (22%)
  waiting for transfers between devices  63.6 us (12%)
  starting transfers between devices  40.8 us (7%)
  local copies, waits for them, and re-layouts  39.4 us (7%)
  other arithmetic  32.2 us (6%)
    psum x1, blocking collectives, per_device(): intersection = lax.psum(partial_intersection, 'node') / total_nodes  247 us
    dot_general x8, matrix products, cell_terms(): jnp.einsum('sjk,jkn->skn', mixed, picker.astype(jnp.float32), precision=l...  82.7 us
    all_to_all x1, waiting for transfers between devices, per_device(): lax.all_to_all(jnp.stack([second] * lax.axis_size('state')), 'state', 0, 0)  41.7 us
    dot_general x8, matrix products, cell_terms(): jnp.einsum('skn,jkn->sjk', part_pair, picker_half, preferred_element_type...  27.9 us
    ppermute x4, starting transfers between devices, passed_along(): return lax.ppermute(block, axis, route)  18.2 us
    ppermute x4, waiting for transfers between devices, passed_along(): return lax.ppermute(block, axis, route)  18 us
    ppermute x2, starting transfers between devices, extended(): lax.ppermute(lax.slice_in_dim(block, 0, width, axis=dim), axis, backward)  13.9 us
  transfers between devices with their start and end apart: 9, of which 7 were waited for; matrix products, arithmetic and copies ran while one was open for 1% of the time, Pallas kernels for 0%

profile of v1, /device:TPU:128, one launch (start us, length us, event | category | flops | bytes accessed | tf_op | source)
XLA Modules:
  0.0 546.2 jit_solution(17650693762845858804)
XLA Ops:
  3.7 7.0 %collective-permute-start.1 = (bf16[16,8192]{1,0:T(8,128)(2,1)S(1)}, bf16[16,8192]{1,0:T(8,128)(2,1)S(1)}, u32[]{:S(2)}, u32[]{:S(2)}) collective-permute-start(bf16[16,8192]{1,0:T(8,128)(2,1)S(1)} %get-tuple-element.59), channel_id=1, source_target_pairs={{4,0},{8,4},{12,8},{16,12},{20,16},{24,20},{28,24},{32,28},{36,32}... | collective-permute-start | bytes 786440 | tf_op jit(solution)/shard_map/ppermute | solution.py:18
  16.1 3.2 reshape.137
  27.7 4.3 fusion.122
  32.8 4.3 fusion.121
  39.0 4.2 fusion.120
  45.0 11.6 %fusion.42 = f32[16,128,192]{2,0,1:T(8,128)S(1)} fusion(s32[125,128]{0,1:T(8,128)S(1)} %copy.16, f32[16,128,125]{2,0,1:T(8,128)S(1)} %copy.33, f32[16,125,128]{1,0,2:T(8,128)} %get-tuple-element.75, f32[125,128]{0,1:T(8,128)} %copy.19), kind=kOutput, calls=%fused_computation.59 | convolution fusion | flops 593408000 | bytes 3748864 | tf_op jit(solution)/shard_map/sjk,jkn->skn/dot_general | solution.py:58
  56.6 9.9 %fusion.44 = f32[16,128,192]{2,0,1:T(8,128)S(1)} fusion(s32[125,128]{0,1:T(8,128)S(1)} %copy-done.11, f32[16,128,125]{2,0,1:T(8,128)S(1)} %copy.35, f32[16,125,128]{1,0,2:T(8,128)S(1)} %copy-done.19, f32[125,128]{0,1:T(8,128)S(1)} %copy-done.14), kind=kOutput, calls=%fused_computation.61 | convolution fusion | flops 593408000 | bytes 3748864 | tf_op jit(solution)/shard_map/sjk,jkn->skn/dot_general | solution.py:58
  66.5 10.0 %fusion.46 = f32[16,128,192]{2,0,1:T(8,128)S(1)} fusion(s32[125,128]{0,1:T(8,128)S(1)} %copy.22, f32[16,128,125]{2,0,1:T(8,128)S(1)} %copy-done.7, f32[16,125,128]{1,0,2:T(8,128)S(1)} %copy-done.20, f32[125,128]{0,1:T(8,128)S(1)} %copy.23), kind=kOutput, calls=%fused_computation.63 | convolution fusion | flops 593408000 | bytes 3748864 | tf_op jit(solution)/shard_map/sjk,jkn->skn/dot_general | solution.py:58
  76.5 9.8 %fusion.48 = f32[16,128,192]{2,0,1:T(8,128)S(1)} fusion(s32[125,128]{0,1:T(8,128)S(1)} %copy.24, f32[16,128,125]{2,0,1:T(8,128)S(1)} %copy-done.9, f32[16,125,128]{1,0,2:T(8,128)S(1)} %copy-done.21, f32[125,128]{0,1:T(8,128)S(1)} %copy.25), kind=kOutput, calls=%fused_computation.65 | convolution fusion | flops 593408000 | bytes 3748864 | tf_op jit(solution)/shard_map/sjk,jkn->skn/dot_general | solution.py:58
  89.7 3.2 copy.26
  93.0 4.0 reshape.138
  97.2 6.9 %collective-permute-start.2 = (bf16[16,8192]{1,0:T(8,128)(2,1)S(1)}, bf16[16,8192]{1,0:T(8,128)(2,1)S(1)}, u32[]{:S(2)}, u32[]{:S(2)}) collective-permute-start(bf16[16,8192]{1,0:T(8,128)(2,1)S(1)} %get-tuple-element.55), channel_id=1, source_target_pairs={{4,0},{8,4},{12,8},{16,12},{20,16},{24,20},{28,24},{32,28},{36,32}... | collective-permute-start | bytes 786440 | tf_op jit(solution)/shard_map/ppermute | solution.py:26
  108.1 8.0 %collective-permute-done.3 = bf16[16,8192]{1,0:T(8,128)(2,1)S(1)} collective-permute-done((bf16[16,8192]{1,0:T(8,128)(2,1)S(1)}, bf16[16,8192]{1,0:T(8,128)(2,1)S(1)}, u32[]{:S(2)}, u32[]{:S(2)}) %collective-permute-start.3) | collective-permute-done | bytes 262176 | tf_op jit(solution)/shard_map/ppermute | solution.py:26
  119.2 7.0 %collective-permute-start.5 = (bf16[16,8192]{1,0:T(8,128)(2,1)S(1)}, bf16[16,8192]{1,0:T(8,128)(2,1)S(1)}, u32[]{:S(2)}, u32[]{:S(2)}) collective-permute-start(bf16[16,8192]{1,0:T(8,128)(2,1)S(1)} %get-tuple-element.57), channel_id=1, source_target_pairs={{4,0},{8,4},{12,8},{16,12},{20,16},{24,20},{28,24},{32,28},{36,32}... | collective-permute-start | bytes 786440 | tf_op jit(solution)/shard_map/ppermute | solution.py:18
  131.3 3.2 reshape.139
  139.2 3.0 fusion.127
  145.3 3.0 fusion.125
  156.7 11.7 %fusion.43 = f32[16,128,192]{2,0,1:T(8,128)S(1)} fusion(s32[125,128]{0,1:T(8,128)S(1)} %copy.16, f32[16,128,125]{2,0,1:T(8,128)} %copy.41, f32[16,125,128]{1,0,2:T(8,128)} %get-tuple-element.83, f32[125,128]{0,1:T(8,128)} %copy.19), kind=kOutput, calls=%fused_computation.60 | convolution fusion | flops 593408000 | bytes 3748864 | tf_op jit(solution)/shard_map/sjk,jkn->skn/dot_general | solution.py:58
  168.4 9.9 %fusion.45 = f32[16,128,192]{2,0,1:T(8,128)S(1)} fusion(s32[125,128]{0,1:T(8,128)S(1)} %copy-done.13, f32[16,128,125]{2,0,1:T(8,128)S(1)} %copy-done.8, f32[16,125,128]{1,0,2:T(8,128)S(1)} %copy-done.18, f32[125,128]{0,1:T(8,128)S(1)} %copy-done.15), kind=kOutput, calls=%fused_computation.62 | convolution fusion | flops 593408000 | bytes 3748864 | tf_op jit(solution)/shard_map/sjk,jkn->skn/dot_general | solution.py:58
  178.3 10.0 %fusion.47 = f32[16,128,192]{2,0,1:T(8,128)S(1)} fusion(s32[125,128]{0,1:T(8,128)S(1)} %copy.22, f32[16,128,125]{2,0,1:T(8,128)S(1)} %copy.45, f32[16,125,128]{1,0,2:T(8,128)S(1)} %copy-done.17, f32[125,128]{0,1:T(8,128)S(1)} %copy.23), kind=kOutput, calls=%fused_computation.64 | convolution fusion | flops 593408000 | bytes 3748864 | tf_op jit(solution)/shard_map/sjk,jkn->skn/dot_general | solution.py:58
  188.3 9.8 %fusion.49 = f32[16,128,192]{2,0,1:T(8,128)S(1)} fusion(s32[125,128]{0,1:T(8,128)S(1)} %copy.24, f32[16,128,125]{2,0,1:T(8,128)S(1)} %copy.47, f32[16,125,128]{1,0,2:T(8,128)S(1)} %copy-done.16, f32[125,128]{0,1:T(8,128)S(1)} %copy.25), kind=kOutput, calls=%fused_computation.66 | convolution fusion | flops 593408000 | bytes 3748864 | tf_op jit(solution)/shard_map/sjk,jkn->skn/dot_general | solution.py:58
  201.6 3.2 copy.29
  204.8 4.0 reshape.140
  209.1 7.3 %collective-permute-start.6 = (bf16[16,8192]{1,0:T(8,128)(2,1)S(1)}, bf16[16,8192]{1,0:T(8,128)(2,1)S(1)}, u32[]{:S(2)}, u32[]{:S(2)}) collective-permute-start(bf16[16,8192]{1,0:T(8,128)(2,1)S(1)} %get-tuple-element.53), channel_id=1, source_target_pairs={{4,0},{8,4},{12,8},{16,12},{20,16},{24,20},{28,24},{32,28},{36,32}... | collective-permute-start | bytes 786440 | tf_op jit(solution)/shard_map/ppermute | solution.py:26
  220.3 7.2 %collective-permute-done.7 = bf16[16,8192]{1,0:T(8,128)(2,1)S(1)} collective-permute-done((bf16[16,8192]{1,0:T(8,128)(2,1)S(1)}, bf16[16,8192]{1,0:T(8,128)(2,1)S(1)}, u32[]{:S(2)}, u32[]{:S(2)}) %collective-permute-start.7) | collective-permute-done | bytes 262176 | tf_op jit(solution)/shard_map/ppermute | solution.py:26
  231.1 4.8 all-to-all-start
  235.9 41.7 %all-to-all-done = bf16[4,16,32768]{2,1,0:T(8,128)(2,1)} async-done(((bf16[4,16,32768]{2,1,0:T(8,128)(2,1)}), bf16[4,16,32768]{2,1,0:T(8,128)(2,1)}, u32[]{:S(2)}, u32[]{:S(2)}) %all-to-all-start) | async-done | bytes 4194336 | tf_op jit(solution)/shard_map/all_to_all | solution.py:105
  277.7 4.7 fusion.128
  282.4 246.6 %psum.7 = f32[64,64]{0,1:T(8,128)S(1)} all-reduce(f32[64,64]{0,1:T(8,128)S(1)} %fusion.128), channel_id=1, replica_groups=mesh['node'=64,'state'=4] {'node'}, use_global_device_ids=true, to_apply=%region_1.0 | all-reduce | flops 4096 | bytes 32768 | tf_op jit(solution)/shard_map/psum | solution.py:108
  529.0 5.8 %cholesky.17 = f32[64,64]{1,0:T(8,128)S(1)} custom-call(f32[64,64]{1,0:T(8,128)S(1)} %fusion.104), custom_call_target="Cholesky" | custom-call | tf_op jit(solution)/shard_map/jit(cholesky)/cholesky | solution.py:87
  536.8 4.9 custom-call.6
  542.0 3.8 convolution_convert_fusion
  (120 shorter events, 66.3 us)
Async XLA Ops:
  0.6 26.2 %copy-start = (bf16[125,125]{1,0:T(8,128)(2,1)S(1)}, bf16[125,125]{1,0:T(8,128)(2,1)}, u32[]{:S(2)}) copy-start(bf16[125,125]{1,0:T(8,128)(2,1)} %param.15) | copy-start | bytes 93754
  0.6 14.1 %copy-start.1 = (bf16[16,32768]{1,0:T(8,128)(2,1)S(1)}, bf16[16,32768]{1,0:T(8,128)(2,1)}, u32[]{:S(2)}) copy-start(bf16[16,32768]{1,0:T(8,128)(2,1)} %param.12) | copy-start | bytes 3145732
  1.8 12.9 %collective-permute-start = (bf16[16,8192]{1,0:T(8,128)(2,1)S(1)}, bf16[16,8192]{1,0:T(8,128)(2,1)S(1)}, u32[]{:S(2)}, u32[]{:S(2)}) collective-permute-start(bf16[16,8192]{1,0:T(8,128)(2,1)S(1)} %get-tuple-element.58), channel_id=1, source_target_pairs={{0,4},{4,8},{8,12},{12,16},{16,20},{20,24},{24,28},{28,32},{32,36}... | collective-permute-start | bytes 786440 | tf_op jit(solution)/shard_map/ppermute | solution.py:15
  3.7 11.0 %collective-permute-start.1 = (bf16[16,8192]{1,0:T(8,128)(2,1)S(1)}, bf16[16,8192]{1,0:T(8,128)(2,1)S(1)}, u32[]{:S(2)}, u32[]{:S(2)}) collective-permute-start(bf16[16,8192]{1,0:T(8,128)(2,1)S(1)} %get-tuple-element.59), channel_id=1, source_target_pairs={{4,0},{8,4},{12,8},{16,12},{20,16},{24,20},{28,24},{32,28},{36,32}... | collective-permute-start | bytes 786440 | tf_op jit(solution)/shard_map/ppermute | solution.py:18
  13.6 14.1 %copy-start.10 = (s32[125,128]{0,1:T(8,128)}, s32[125,128]{0,1:T(8,128)S(1)}, u32[]{:S(2)}) copy-start(s32[125,128]{0,1:T(8,128)S(1)} %copy.20) | copy-start | bytes 192004
  23.8 3.0 copy-start.6
  45.0 11.6 %copy-start.11 = (s32[125,128]{0,1:T(8,128)S(1)}, s32[125,128]{0,1:T(8,128)}, u32[]{:S(2)}) copy-start(s32[125,128]{0,1:T(8,128)} %copy-done.10) | copy-start | bytes 192004
  45.0 11.6 %copy-start.14 = (f32[125,128]{0,1:T(8,128)S(1)}, f32[125,128]{0,1:T(8,128)}, u32[]{:S(2)}) copy-start(f32[125,128]{0,1:T(8,128)} %copy.21) | copy-start | bytes 192004
  45.0 11.6 %copy-start.19 = (f32[16,125,128]{1,0,2:T(8,128)S(1)}, f32[16,125,128]{1,0,2:T(8,128)}, u32[]{:S(2)}) copy-start(f32[16,125,128]{1,0,2:T(8,128)} %get-tuple-element.73) | copy-start | bytes 3072004
  56.6 9.9 %copy-start.7 = (f32[16,128,125]{2,0,1:T(8,128)S(1)}, f32[16,128,125]{2,0,1:T(8,128)}, u32[]{:S(2)}) copy-start(f32[16,128,125]{2,0,1:T(8,128)} %copy.37) | copy-start | bytes 3072004
  56.6 9.9 %copy-start.20 = (f32[16,125,128]{1,0,2:T(8,128)S(1)}, f32[16,125,128]{1,0,2:T(8,128)}, u32[]{:S(2)}) copy-start(f32[16,125,128]{1,0,2:T(8,128)} %get-tuple-element.71) | copy-start | bytes 3072004
  66.5 10.0 %copy-start.9 = (f32[16,128,125]{2,0,1:T(8,128)S(1)}, f32[16,128,125]{2,0,1:T(8,128)}, u32[]{:S(2)}) copy-start(f32[16,128,125]{2,0,1:T(8,128)} %copy.39) | copy-start | bytes 3072004
  66.5 10.0 %copy-start.21 = (f32[16,125,128]{1,0,2:T(8,128)S(1)}, f32[16,125,128]{1,0,2:T(8,128)}, u32[]{:S(2)}) copy-start(f32[16,125,128]{1,0,2:T(8,128)} %get-tuple-element.69) | copy-start | bytes 3072004
  97.2 10.8 %collective-permute-start.2 = (bf16[16,8192]{1,0:T(8,128)(2,1)S(1)}, bf16[16,8192]{1,0:T(8,128)(2,1)S(1)}, u32[]{:S(2)}, u32[]{:S(2)}) collective-permute-start(bf16[16,8192]{1,0:T(8,128)(2,1)S(1)} %get-tuple-element.55), channel_id=1, source_target_pairs={{4,0},{8,4},{12,8},{16,12},{20,16},{24,20},{28,24},{32,28},{36,32}... | collective-permute-start | bytes 786440 | tf_op jit(solution)/shard_map/ppermute | solution.py:26
  104.8 12.1 %copy-start.2 = (bf16[16,32768]{1,0:T(8,128)(2,1)S(1)}, bf16[16,32768]{1,0:T(8,128)(2,1)}, u32[]{:S(2)}) copy-start(bf16[16,32768]{1,0:T(8,128)(2,1)} %param.12) | copy-start | bytes 3145732
  104.9 11.1 %collective-permute-start.3 = (bf16[16,8192]{1,0:T(8,128)(2,1)S(1)}, bf16[16,8192]{1,0:T(8,128)(2,1)S(1)}, u32[]{:S(2)}, u32[]{:S(2)}) collective-permute-start(bf16[16,8192]{1,0:T(8,128)(2,1)S(1)} %get-tuple-element.54), channel_id=1, source_target_pairs={{0,4},{4,8},{8,12},{12,16},{16,20},{20,24},{24,28},{28,32},{32,36}... | collective-permute-start | bytes 786440 | tf_op jit(solution)/shard_map/ppermute | solution.py:26
  117.2 12.8 %copy-start.4 = (bf16[16,32768]{1,0:T(8,128)(2,1)}, bf16[16,32768]{1,0:T(8,128)(2,1)S(1)}, u32[]{:S(2)}) copy-start(bf16[16,32768]{1,0:T(8,128)(2,1)S(1)} %fusion.40) | copy-start | bytes 3145732
  117.3 11.0 %collective-permute-start.4 = (bf16[16,8192]{1,0:T(8,128)(2,1)S(1)}, bf16[16,8192]{1,0:T(8,128)(2,1)S(1)}, u32[]{:S(2)}, u32[]{:S(2)}) collective-permute-start(bf16[16,8192]{1,0:T(8,128)(2,1)S(1)} %get-tuple-element.56), channel_id=1, source_target_pairs={{0,4},{4,8},{8,12},{12,16},{16,20},{20,24},{24,28},{28,32},{32,36}... | collective-permute-start | bytes 786440 | tf_op jit(solution)/shard_map/ppermute | solution.py:15
  119.2 10.8 %collective-permute-start.5 = (bf16[16,8192]{1,0:T(8,128)(2,1)S(1)}, bf16[16,8192]{1,0:T(8,128)(2,1)S(1)}, u32[]{:S(2)}, u32[]{:S(2)}) collective-permute-start(bf16[16,8192]{1,0:T(8,128)(2,1)S(1)} %get-tuple-element.57), channel_id=1, source_target_pairs={{4,0},{8,4},{12,8},{16,12},{20,16},{24,20},{28,24},{32,28},{36,32}... | collective-permute-start | bytes 786440 | tf_op jit(solution)/shard_map/ppermute | solution.py:18
  139.2 3.1 copy-start.12
  156.6 11.7 %copy-start.8 = (f32[16,128,125]{2,0,1:T(8,128)S(1)}, f32[16,128,125]{2,0,1:T(8,128)}, u32[]{:S(2)}) copy-start(f32[16,128,125]{2,0,1:T(8,128)} %copy.43) | copy-start | bytes 3072004
  156.6 11.7 %copy-start.13 = (s32[125,128]{0,1:T(8,128)S(1)}, s32[125,128]{0,1:T(8,128)}, u32[]{:S(2)}) copy-start(s32[125,128]{0,1:T(8,128)} %copy-done.10) | copy-start | bytes 192004
  156.6 11.7 %copy-start.15 = (f32[125,128]{0,1:T(8,128)S(1)}, f32[125,128]{0,1:T(8,128)}, u32[]{:S(2)}) copy-start(f32[125,128]{0,1:T(8,128)} %copy.21) | copy-start | bytes 192004
  156.7 11.7 %copy-start.18 = (f32[16,125,128]{1,0,2:T(8,128)S(1)}, f32[16,125,128]{1,0,2:T(8,128)}, u32[]{:S(2)}) copy-start(f32[16,125,128]{1,0,2:T(8,128)} %get-tuple-element.81) | copy-start | bytes 3072004
  168.4 9.9 %copy-start.17 = (f32[16,125,128]{1,0,2:T(8,128)S(1)}, f32[16,125,128]{1,0,2:T(8,128)}, u32[]{:S(2)}) copy-start(f32[16,125,128]{1,0,2:T(8,128)} %get-tuple-element.79) | copy-start | bytes 3072004
  178.3 10.1 %copy-start.16 = (f32[16,125,128]{1,0,2:T(8,128)S(1)}, f32[16,125,128]{1,0,2:T(8,128)}, u32[]{:S(2)}) copy-start(f32[16,125,128]{1,0,2:T(8,128)} %get-tuple-element.77) | copy-start | bytes 3072004
  209.0 19.3 %copy-start.3 = (bf16[16,32768]{1,0:T(8,128)(2,1)S(1)}, bf16[16,32768]{1,0:T(8,128)(2,1)}, u32[]{:S(2)}) copy-start(bf16[16,32768]{1,0:T(8,128)(2,1)} %param.12) | copy-start | bytes 3145732
  209.1 19.3 %copy-start.5 = (bf16[16,32768]{1,0:T(8,128)(2,1)S(1)}, bf16[16,32768]{1,0:T(8,128)(2,1)}, u32[]{:S(2)}) copy-start(bf16[16,32768]{1,0:T(8,128)(2,1)} %copy-done.4) | copy-start | bytes 3145732
  209.1 11.1 %collective-permute-start.6 = (bf16[16,8192]{1,0:T(8,128)(2,1)S(1)}, bf16[16,8192]{1,0:T(8,128)(2,1)S(1)}, u32[]{:S(2)}, u32[]{:S(2)}) collective-permute-start(bf16[16,8192]{1,0:T(8,128)(2,1)S(1)} %get-tuple-element.53), channel_id=1, source_target_pairs={{4,0},{8,4},{12,8},{16,12},{20,16},{24,20},{28,24},{32,28},{36,32}... | collective-permute-start | bytes 786440 | tf_op jit(solution)/shard_map/ppermute | solution.py:26
  216.5 11.0 %collective-permute-start.7 = (bf16[16,8192]{1,0:T(8,128)(2,1)S(1)}, bf16[16,8192]{1,0:T(8,128)(2,1)S(1)}, u32[]{:S(2)}, u32[]{:S(2)}) collective-permute-start(bf16[16,8192]{1,0:T(8,128)(2,1)S(1)} %get-tuple-element.52), channel_id=1, source_target_pairs={{0,4},{4,8},{8,12},{12,16},{16,20},{20,24},{24,28},{28,32},{32,36}... | collective-permute-start | bytes 786440 | tf_op jit(solution)/shard_map/ppermute | solution.py:26
  231.1 46.6 %all-to-all-start = ((bf16[4,16,32768]{2,1,0:T(8,128)(2,1)}), bf16[4,16,32768]{2,1,0:T(8,128)(2,1)}, u32[]{:S(2)}, u32[]{:S(2)}) async-start(bf16[4,16,32768]{2,1,0:T(8,128)(2,1)} %stack.2), calls=%async_computation | async-start | bytes 8388608 | tf_op jit(solution)/shard_map/all_to_all | solution.py:105
